TPU v7x, 32 devices: a whole 2x2x4 slice. The times are simulated.
32 devices in a mesh: row: 4 (over z), col: 8 (over y, x, core).
Axes of the slice: x: 2, y: 2, z: 4, core: 2. Of those that a mesh axis runs over, the one named last changes fastest.
Arguments:
- state_start: bfloat16 [512, 2048], P('row', 'col'), may hold values from -360 to 360
- actions: int32 [512, 2], P('row'), may hold values from 0 to 17
- targets: bfloat16 [2, 512, 2048], P(None, 'row'), may hold values from -504 to 504
- w_in: bfloat16 [2048, 4096], P('row', 'col'), may hold values from -0.125 to 0.125
- w_out: bfloat16 [4096, 2048], P('col', 'row'), may hold values from -0.09375 to 0.09375
- action_embed: bfloat16 [18, 4096], P(None, 'col'), may hold values from -6 to 6
Outputs:
- grad_w_in: float32 [2048, 4096], P('row', 'col')
- grad_w_out: float32 [4096, 2048], P('col', 'row')
All inputs are finite; a program needn't handle non-finite values.
Results may differ from a plain program's by a relative error of at most 0.035.
Values may be sent and summed in bfloat16 or wider, within the bound.
A program may use at most 64 MiB of HBM per device.

v0:
```python
import jax
import jax.numpy as jnp
from jax import lax
from jax.sharding import PartitionSpec as P

EPS = 1e-06
LOSS_SCALE = 128.0


def silu_grad(pre_act):
    gate_val = jax.nn.sigmoid(pre_act)
    return gate_val * (1.0 + pre_act * (1.0 - gate_val))


def cosine_from(state_f, target_f, self_dot, cross_dot, target_dot):
    inv_state = lax.rsqrt(self_dot + EPS)
    inv_target = lax.rsqrt(target_dot + EPS)
    cosine = cross_dot * inv_state * inv_target
    return -LOSS_SCALE * (
        target_f * inv_state * inv_target - cosine * state_f * inv_state * inv_state
    )


def shared_cosine(state, target):
    state_f = state.astype(jnp.float32)
    target_f = target.astype(jnp.float32)
    self_dot, cross_dot, target_dot = lax.psum(
        (
            jnp.sum(state_f * state_f, axis=-1),
            jnp.sum(state_f * target_f, axis=-1),
            jnp.sum(target_f * target_f, axis=-1),
        ),
        "col",
    )
    return cosine_from(
        state_f, target_f, self_dot[:, None], cross_dot[:, None], target_dot[:, None]
    )


def on_device(state_start, actions, targets, w_in, w_out, action_embed):
    unroll_steps = targets.shape[0]
    col_width = state_start.shape[1]
    w_in_panel = lax.all_gather(w_in, "row", axis=0, tiled=True)
    w_out_panel = lax.all_gather(w_out, "row", axis=1, tiled=True)
    col_start = lax.axis_index("col") * col_width
    action_ids = jnp.arange(action_embed.shape[0], dtype=jnp.int32)
    contract_last = (((1,), (1,)), ((), ()))
    current = state_start
    full_states = []
    pre_list = []
    hidden_list = []
    cos_terms = []
    for unroll in range(unroll_steps):
        full_rows = lax.all_gather(current, "col", axis=1, tiled=True)
        onehot = (actions[:, unroll][:, None] == action_ids[None, :]).astype(jnp.bfloat16)
        pre_act = jnp.dot(full_rows, w_in_panel, preferred_element_type=jnp.float32) + jnp.dot(
            onehot, action_embed, preferred_element_type=jnp.float32
        )
        hidden = jax.nn.silu(pre_act).astype(jnp.bfloat16)
        partial_value = jnp.dot(hidden, w_out_panel, preferred_element_type=jnp.float32)
        target = targets[unroll]
        branch = lax.psum_scatter(
            partial_value.astype(jnp.bfloat16), "col", scatter_dimension=1, tiled=True
        ).astype(jnp.float32)
        current = (current.astype(jnp.float32) + branch).astype(jnp.bfloat16)
        target_slice = lax.dynamic_slice_in_dim(target, col_start, col_width, 1)
        cos_terms.append(shared_cosine(current, target_slice))
        full_states.append(full_rows)
        pre_list.append(pre_act)
        hidden_list.append(hidden)
    state_grad = cos_terms[unroll_steps - 1].astype(jnp.bfloat16)
    grad_list = [None] * unroll_steps
    hid_grads = [None] * unroll_steps
    for unroll in reversed(range(unroll_steps)):
        grad_rows = lax.all_gather(state_grad, "col", axis=1, tiled=True)
        back = lax.dot_general(
            grad_rows, w_out_panel, contract_last, preferred_element_type=jnp.float32
        )
        hid_grad = (back * silu_grad(pre_list[unroll])).astype(jnp.bfloat16)
        grad_list[unroll] = grad_rows
        hid_grads[unroll] = hid_grad
        if unroll > 0:
            input_part = lax.dot_general(
                hid_grad, w_in_panel, contract_last, preferred_element_type=jnp.float32
            )
            summed = lax.psum_scatter(
                input_part.astype(jnp.bfloat16), "col", scatter_dimension=1, tiled=True
            ).astype(jnp.float32)
            state_grad = (state_grad.astype(jnp.float32) + summed + cos_terms[unroll - 1]).astype(
                jnp.bfloat16
            )
    grad_stack = jnp.stack(grad_list)
    hidden_stack = jnp.stack(hidden_list)
    state_stack = jnp.stack(full_states)
    hid_stack = jnp.stack(hid_grads)
    grad_feature_blocks = lax.all_to_all(grad_stack, "row", split_axis=2, concat_axis=1, tiled=True)
    hidden_all = lax.all_gather(hidden_stack, "row", axis=1, tiled=True)
    grad_w_out = jnp.einsum(
        "kbf,kbd->fd", hidden_all, grad_feature_blocks, preferred_element_type=jnp.float32
    )
    state_feature_blocks = lax.all_to_all(
        state_stack, "row", split_axis=2, concat_axis=1, tiled=True
    )
    hid_all = lax.all_gather(hid_stack, "row", axis=1, tiled=True)
    grad_w_in = jnp.einsum(
        "kbd,kbf->df", state_feature_blocks, hid_all, preferred_element_type=jnp.float32
    )
    return (grad_w_in, grad_w_out)


def solution(mesh):
    in_specs = (
        P("row", "col"),
        P("row", None),
        P(None, "row", None),
        P("row", "col"),
        P("col", "row"),
        P(None, "col"),
    )
    out_specs = (P("row", "col"), P("col", "row"))
    return jax.shard_map(
        on_device, mesh=mesh, in_specs=in_specs, out_specs=out_specs, check_vma=False
    )
```

profile of v0, /device:TPU:0, one launch (start us, length us, event | category | flops | bytes accessed | tf_op | source)
XLA Modules:
  0.0 336.0 jit_solution(11510671725148091114)
XLA Ops:
  8.7 12.7 %all_gather.24 = bf16[128,2048]{1,0:T(8,128)(2,1)S(1)} all-gather(bf16[128,256]{1,0:T(8,128)(2,1)} %param.6), channel_id=1, replica_groups=mesh['row'=4,'col'=8] {'col'}, dimensions={1}, use_global_device_ids=true | all-gather | bytes 589824 | tf_op jit(solution)/shard_map/all_gather | solution.py:54
  22.4 35.6 %all-gather.5.cloned.1.call-done = bf16[2048,512]{1,0:T(8,128)(2,1)} async-done(((bf16[512,512]{1,0:T(8,128)(2,1)}), bf16[2048,512]{1,0:T(8,128)(2,1)}) %all-gather.5.cloned.1.call-update) | async-done | bytes 2097168 | tf_op jit(solution)/shard_map/all_gather | solution.py:43
  58.0 2.0 convolution_add_fusion.1
  60.0 44.0 %all-gather.7.cloned.1.call-done = bf16[512,2048]{1,0:T(8,128)(2,1)} async-done(((bf16[512,512]{1,0:T(8,128)(2,1)}), bf16[512,2048]{1,0:T(8,128)(2,1)}) %all-gather.7.cloned.1.call-update) | async-done | bytes 2097168 | tf_op jit(solution)/shard_map/all_gather | solution.py:44
  104.0 2.9 convolution_convert_fusion.2
  107.0 1.0 fusion.24
  107.9 2.1 fusion.29
  110.0 30.6 %reduce-scatter.4.cloned.1.call-done = bf16[128,256]{1,0:T(8,128)(2,1)} async-done(((bf16[128,2048]{1,0:T(8,128)(2,1)}), bf16[128,256]{1,0:T(8,128)(2,1)}) %reduce-scatter.4.cloned.1.call-update) | async-done | bytes 65552 | tf_op jit(solution)/shard_map/reduce_scatter | solution.py:62
  140.6 1.1 fusion.17
  141.8 10.9 %all_gather.27 = bf16[128,2048]{1,0:T(8,128)(2,1)S(1)} all-gather(bf16[128,256]{1,0:T(8,128)(2,1)S(1)} %get-tuple-element.14), channel_id=1, replica_groups=mesh['row'=4,'col'=8] {'col'}, dimensions={1}, use_global_device_ids=true | all-gather | bytes 589824 | tf_op jit(solution)/shard_map/all_gather | solution.py:54
  152.7 2.1 convolution_add_fusion
  154.8 2.2 convolution_convert_fusion.1
  157.1 34.2 %reduce-scatter.6.cloned.1.call-done = bf16[128,256]{1,0:T(8,128)(2,1)} async-done(((bf16[128,2048]{1,0:T(8,128)(2,1)}), bf16[128,256]{1,0:T(8,128)(2,1)}) %reduce-scatter.6.cloned.1.call-update) | async-done | bytes 65552 | tf_op jit(solution)/shard_map/reduce_scatter | solution.py:62
  191.3 1.0 fusion.10
  192.3 12.1 %all-reduce = (f32[128]{0:T(128)S(1)}, f32[128]{0:T(128)S(1)}, f32[128]{0:T(128)S(1)}, f32[128]{0:T(128)S(1)}, f32[128]{0:T(128)S(1)}, /*index=5*/f32[128]{0:T(128)S(1)}) all-reduce(f32[128]{0:T(128)S(1)} %get-tuple-element.5, f32[128]{0:T(128)S(1)} %get-tuple-element.6, ...), channel_id=1, replica_groups=mesh['row'=4,'col'=8] {'col'}, use_global_device_ids=true, to_apply=%region_7.8 | all-reduce | flops 768 | bytes 6144 | tf_op jit(solution)/shard_map/psum | solution.py:27
  204.5 1.0 fusion.8
  206.1 10.9 %all_gather.28 = bf16[128,2048]{1,0:T(8,128)(2,1)S(1)} all-gather(bf16[128,256]{1,0:T(8,128)(2,1)S(1)} %fusion.8), channel_id=1, replica_groups=mesh['row'=4,'col'=8] {'col'}, dimensions={1}, use_global_device_ids=true | all-gather | bytes 589824 | tf_op jit(solution)/shard_map/all_gather | solution.py:75
  217.8 2.4 fusion
  220.9 1.6 convolution_convert_fusion
  222.6 2.0 copy.11
  224.6 4.9 %all-to-all-start = ((bf16[2,128,2048]{1,0,2:T(2,128)(2,1)}), bf16[2,128,2048]{1,0,2:T(2,128)(2,1)S(1)}, u32[]{:S(2)}, u32[]{:S(2)}) async-start(bf16[2,128,2048]{1,0,2:T(2,128)(2,1)} %copy.11), calls=%async_computation.1 | async-start | bytes 2097152 | tf_op jit(solution)/shard_map/all_to_all | solution.py:101
  229.6 1.0 fusion.28
  231.4 25.5 %reduce-scatter.8.cloned.1.call-done = bf16[128,256]{1,0:T(8,128)(2,1)} async-done(((bf16[128,2048]{1,0:T(8,128)(2,1)}), bf16[128,256]{1,0:T(8,128)(2,1)}) %reduce-scatter.8.cloned.1.call-update) | async-done | bytes 65552 | tf_op jit(solution)/shard_map/reduce_scatter | solution.py:86
  256.9 1.0 fusion.16
  258.0 10.9 %all_gather.29 = bf16[128,2048]{1,0:T(8,128)(2,1)S(1)} all-gather(bf16[128,256]{1,0:T(8,128)(2,1)S(1)} %fusion.16), channel_id=1, replica_groups=mesh['row'=4,'col'=8] {'col'}, dimensions={1}, use_global_device_ids=true | all-gather | bytes 589824 | tf_op jit(solution)/shard_map/all_gather | solution.py:75
  269.0 2.0 copy.13
  271.0 4.6 %all-to-all-start.1 = ((bf16[2,128,2048]{1,0,2:T(2,128)(2,1)}), bf16[2,128,2048]{1,0,2:T(2,128)(2,1)S(1)}, u32[]{:S(2)}, u32[]{:S(2)}) async-start(bf16[2,128,2048]{1,0,2:T(2,128)(2,1)} %copy.13), calls=%async_computation.4 | async-start | bytes 2097152 | tf_op jit(solution)/shard_map/all_to_all | solution.py:96
  275.6 2.5 fusion.2
  280.1 33.4 %all-to-all-done.1 = bf16[2,128,2048]{1,0,2:T(2,128)(2,1)S(1)} async-done(((bf16[2,128,2048]{1,0,2:T(2,128)(2,1)}), bf16[2,128,2048]{1,0,2:T(2,128)(2,1)S(1)}, u32[]{:S(2)}, u32[]{:S(2)}) %all-to-all-start.1) | async-done | bytes 1048608 | tf_op jit(solution)/shard_map/all_to_all | solution.py:96
  314.3 2.9 convolution_bitcast_fusion
  317.2 9.0 %all-gather.9.cloned.1.call-done = bf16[2,512,512]{2,1,0:T(8,128)(2,1)} async-done(((bf16[2,128,512]{2,1,0:T(8,128)(2,1)}), bf16[2,512,512]{2,1,0:T(8,128)(2,1)}) %all-gather.9.cloned.1.call-update) | async-done | bytes 1048592 | tf_op jit(solution)/shard_map/all_gather | solution.py:104
  326.2 2.9 convolution_bitcast_fusion.1
  (48 shorter events, 8.6 us)
Async XLA Ops:
  7.2 15.0 %copy-start = (bf16[18,512]{1,0:T(8,128)(2,1)S(1)}, bf16[18,512]{1,0:T(8,128)(2,1)}, u32[]{:S(2)}) copy-start(bf16[18,512]{1,0:T(8,128)(2,1)} %param.11) | copy-start | bytes 55300
  7.2 50.8 %all-gather.5.cloned.1.call-start = ((), (), s32[]{:S(2)}) async-start(), calls=%async_computation.5 | async-start | bytes 2621440 | tf_op jit(solution)/shard_map/all_gather | solution.py:43
  7.9 96.1 %all-gather.7.cloned.1.call-start = ((), (), s32[]{:S(2)}) async-start(), calls=%async_computation.6 | async-start | bytes 2621440 | tf_op jit(solution)/shard_map/all_gather | solution.py:44
  8.7 132.0 %reduce-scatter.4.cloned.1.call-start = ((), (), s32[]{:S(2)}) async-start(), calls=%async_computation.7 | async-start | bytes 589824 | tf_op jit(solution)/shard_map/reduce_scatter | solution.py:62
  106.9 45.8 %copy-start.1 = (bf16[2048,512]{1,0:T(8,128)(2,1)S(1)}, bf16[2048,512]{1,0:T(8,128)(2,1)}, u32[]{:S(2)}) copy-start(bf16[2048,512]{1,0:T(8,128)(2,1)} %all-gather.5.cloned.1.call-done) | copy-start | bytes 6291460
  106.9 84.4 %reduce-scatter.6.cloned.1.call-start = ((), (), s32[]{:S(2)}) async-start(), calls=%async_computation.8 | async-start | bytes 589824 | tf_op jit(solution)/shard_map/reduce_scatter | solution.py:62
  110.0 31.7 %copy-start.4 = (bf16[1,128,2048]{2,1,0:T(8,128)(2,1)}, bf16[1,128,2048]{2,1,0:T(8,128)(2,1)S(1)}, u32[]{:S(2)}) copy-start(bf16[1,128,2048]{2,1,0:T(8,128)(2,1)S(1)} %get-tuple-element.16) | copy-start | bytes 1572868
  140.6 14.2 %copy-start.9 = (bf16[512,2048]{1,0:T(8,128)(2,1)S(1)}, bf16[512,2048]{1,0:T(8,128)(2,1)}, u32[]{:S(2)}) copy-start(bf16[512,2048]{1,0:T(8,128)(2,1)} %all-gather.7.cloned.1.call-done) | copy-start | bytes 6291460
  157.0 99.9 %reduce-scatter.8.cloned.1.call-start = ((), (), s32[]{:S(2)}) async-start(), calls=%async_computation.9 | async-start | bytes 589824 | tf_op jit(solution)/shard_map/reduce_scatter | solution.py:86
  205.5 0.6 copy-start.5
  217.0 0.8 copy-start.2
  220.2 0.6 copy-start.7
  224.6 32.3 %copy-start.6 = (bf16[128,256]{1,0:T(8,128)(2,1)S(1)}, bf16[128,256]{1,0:T(8,128)(2,1)}, u32[]{:S(2)}) copy-start(bf16[128,256]{1,0:T(8,128)(2,1)} %copy-done.5) | copy-start | bytes 196612
  224.6 44.2 %copy-start.3 = (bf16[128,2048]{1,0:T(8,128)(2,1)S(1)}, bf16[128,2048]{1,0:T(8,128)(2,1)}, u32[]{:S(2)}) copy-start(bf16[128,2048]{1,0:T(8,128)(2,1)} %copy-done.2) | copy-start | bytes 1572868
  224.6 46.3 %all-to-all-start = ((bf16[2,128,2048]{1,0,2:T(2,128)(2,1)}), bf16[2,128,2048]{1,0,2:T(2,128)(2,1)S(1)}, u32[]{:S(2)}, u32[]{:S(2)}) async-start(bf16[2,128,2048]{1,0,2:T(2,128)(2,1)} %copy.11), calls=%async_computation.1 | async-start | bytes 2097152 | tf_op jit(solution)/shard_map/all_to_all | solution.py:101
  229.5 84.8 %all-gather.11.cloned.1.call-start = ((), (), s32[]{:S(2)}) async-start(), calls=%async_computation.11 | async-start | bytes 1310720 | tf_op jit(solution)/shard_map/all_gather | solution.py:97
  271.0 42.5 %all-to-all-start.1 = ((bf16[2,128,2048]{1,0,2:T(2,128)(2,1)}), bf16[2,128,2048]{1,0,2:T(2,128)(2,1)S(1)}, u32[]{:S(2)}, u32[]{:S(2)}) async-start(bf16[2,128,2048]{1,0,2:T(2,128)(2,1)} %copy.13), calls=%async_computation.4 | async-start | bytes 2097152 | tf_op jit(solution)/shard_map/all_to_all | solution.py:96
  275.6 2.5 copy-start.8
  275.6 50.7 %all-gather.9.cloned.1.call-start = ((), (), s32[]{:S(2)}) async-start(), calls=%async_computation.10 | async-start | bytes 1310720 | tf_op jit(solution)/shard_map/all_gather | solution.py:104
Sparse Core Ops, SparseCore 0:
  9.6 48.3 all-gather.4
  59.5 44.4 all-gather.6
  107.7 32.8 reduce-scatter.3
  157.1 34.0 reduce-scatter.5
  222.6 34.2 reduce-scatter.7
  258.4 37.5 all-gather.10
  297.5 28.6 all-gather.8
where the time goes:
time: 337 us; the launch traced here: 336 us
  waiting for transfers between devices  214 us (64%)
  blocking collectives  57.5 us (17%)
  matrix products  22.8 us (7%)
  between operations  14.3 us (4%)
  local copies, waits for them, and re-layouts  11 us (3%)
  starting transfers between devices  9.7 us (3%)
  other arithmetic  6.97 us (2%)
    reduce_scatter x2, waiting for transfers between devices, on_device(): lax.psum_scatter(partial_value.astype(jnp.bfloat16), 'col', scatter_dimen...  64.8 us
    all_gather x1, waiting for transfers between devices, on_device(): w_out_panel = lax.all_gather(w_out, 'row', axis=1, tiled=True)  44 us
    all_gather x1, waiting for transfers between devices, on_device(): w_in_panel = lax.all_gather(w_in, 'row', axis=0, tiled=True)  35.6 us
    all_to_all x1, waiting for transfers between devices, on_device(): lax.all_to_all(grad_stack, 'row', split_axis=2, concat_axis=1, tiled=True)  33.4 us
    reduce_scatter x1, waiting for transfers between devices, on_device(): lax.psum_scatter(input_part.astype(jnp.bfloat16), 'col', scatter_dimensio...  25.5 us
    all_gather x2, blocking collectives, on_device(): full_rows = lax.all_gather(current, 'col', axis=1, tiled=True)  23.6 us
    all_gather x2, blocking collectives, on_device(): grad_rows = lax.all_gather(state_grad, 'col', axis=1, tiled=True)  21.8 us
    psum x1, blocking collectives, shared_cosine(): lax.psum((jnp.sum(state_f * state_f, axis=-1), jnp.sum(state_f * target_f...  12.1 us
  transfers between devices with their start and end apart: 9, of which 7 were waited for; matrix products, arithmetic and copies ran while one was open for 6% of the time, Pallas kernels for 0%

commit v1 on v0

--- a/solution.py
+++ b/solution.py
@@ -51,7 +51,17 @@
     hidden_list = []
     cos_terms = []
     for unroll in range(unroll_steps):
-        full_rows = lax.all_gather(current, "col", axis=1, tiled=True)
+        carry, base_arr = (lax.axis_size("col"), lax.axis_index("col"))
+        full_rows, w_next = (current, 1)
+        while w_next < carry:
+            heap = []
+            for u in range(carry):
+                heap.append((u, u ^ w_next))
+            all_rows = lax.ppermute(full_rows, "col", heap)
+            b_now = jnp.concatenate([full_rows, all_rows], axis=1)
+            v1 = jnp.concatenate([all_rows, full_rows], axis=1)
+            full_rows = jnp.where(base_arr & w_next == 0, b_now, v1)
+            w_next = 2 * w_next
         onehot = (actions[:, unroll][:, None] == action_ids[None, :]).astype(jnp.bfloat16)
         pre_act = jnp.dot(full_rows, w_in_panel, preferred_element_type=jnp.float32) + jnp.dot(
             onehot, action_embed, preferred_element_type=jnp.float32

time: 337 us -> 336 us (level)
  blocking collectives: 57.5 us -> 33.9 us
  waiting for transfers between devices: 214 us -> 231 us
  starting transfers between devices: 9.7 us -> 18 us
  matrix products: 22.8 us -> 19.4 us
    all_gather x2 -> x0, blocking collectives: 23.6 us -> none  [on_device(): full_rows = lax.all_gather(current, 'col', axis=1, tiled=True)]
    ppermute x0 -> x6, waiting for transfers between devices: none -> 21.1 us  [on_device(): all_rows = lax.ppermute(full_rows, 'col', heap)]
    ppermute x0 -> x6, starting transfers between devices: none -> 8.42 us  [on_device(): all_rows = lax.ppermute(full_rows, 'col', heap)]
    all_gather x1, waiting for transfers between devices: 35.6 us -> 32 us  [on_device(): w_in_panel = lax.all_gather(w_in, 'row', axis=0, tiled=True)]
  transfers between devices with their start and end apart: 9 -> 15, of which waited for: 7 -> 13; matrix products, arithmetic and copies ran while one was open for 6% -> 7% of each run, Pallas kernels for 0% -> 0%
where the time goes in v1:
time: 336 us; the launch traced here: 335 us
  waiting for transfers between devices  231 us (69%)
  blocking collectives  33.9 us (10%)
  matrix products  19.4 us (6%)
  starting transfers between devices  18 us (5%)
  between operations  14.4 us (4%)
  other arithmetic  10.2 us (3%)
  local copies, waits for them, and re-layouts  8.82 us (3%)
    reduce_scatter x2, waiting for transfers between devices, on_device(): lax.psum_scatter(partial_value.astype(jnp.bfloat16), 'col', scatter_dimen...  64.1 us
    all_gather x1, waiting for transfers between devices, on_device(): w_out_panel = lax.all_gather(w_out, 'row', axis=1, tiled=True)  44 us
    all_to_all x1, waiting for transfers between devices, on_device(): lax.all_to_all(grad_stack, 'row', split_axis=2, concat_axis=1, tiled=True)  33.5 us
    all_gather x1, waiting for transfers between devices, on_device(): w_in_panel = lax.all_gather(w_in, 'row', axis=0, tiled=True)  32 us
    reduce_scatter x1, waiting for transfers between devices, on_device(): lax.psum_scatter(input_part.astype(jnp.bfloat16), 'col', scatter_dimensio...  25.6 us
    all_gather x2, blocking collectives, on_device(): grad_rows = lax.all_gather(state_grad, 'col', axis=1, tiled=True)  21.8 us
    ppermute x6, waiting for transfers between devices, on_device(): all_rows = lax.ppermute(full_rows, 'col', heap)  21.1 us
    psum x1, blocking collectives, shared_cosine(): lax.psum((jnp.sum(state_f * state_f, axis=-1), jnp.sum(state_f * target_f...  12.2 us
  transfers between devices with their start and end apart: 15, of which 13 were waited for; matrix products, arithmetic and copies ran while one was open for 7% of the time, Pallas kernels for 0%

profile of v1, /device:TPU:0, one launch (start us, length us, event | category | flops | bytes accessed | tf_op | source)
XLA Modules:
  0.0 335.3 jit_solution(4647112681859282861)
XLA Ops:
  11.3 2.9 collective-permute-start.1
  14.2 3.8 %collective-permute-done.1 = bf16[128,512]{1,0:T(8,128)(2,1)S(1)} collective-permute-done((bf16[128,512]{1,0:T(8,128)(2,1)S(1)}, bf16[128,512]{1,0:T(8,128)(2,1)S(1)}, u32[]{:S(2)}, u32[]{:S(2)}) %collective-permute-start.1) | collective-permute-done | bytes 131104 | tf_op jit(solution)/shard_map/ppermute | solution.py:60
  18.1 1.8 collective-permute-start.2
  21.0 5.0 %collective-permute-done.2 = bf16[128,1024]{1,0:T(8,128)(2,1)S(1)} collective-permute-done((bf16[128,1024]{1,0:T(8,128)(2,1)S(1)}, bf16[128,1024]{1,0:T(8,128)(2,1)S(1)}, u32[]{:S(2)}, u32[]{:S(2)}) %collective-permute-start.2) | collective-permute-done | bytes 262176 | tf_op jit(solution)/shard_map/ppermute | solution.py:60
  26.0 32.0 %all-gather.5.cloned.1.call-done = bf16[2048,512]{1,0:T(8,128)(2,1)} async-done(((bf16[512,512]{1,0:T(8,128)(2,1)}), bf16[2048,512]{1,0:T(8,128)(2,1)}) %all-gather.5.cloned.1.call-update) | async-done | bytes 2097168 | tf_op jit(solution)/shard_map/all_gather | solution.py:43
  58.0 2.0 convolution_add_fusion.1
  60.0 44.0 %all-gather.7.cloned.1.call-done = bf16[512,2048]{1,0:T(8,128)(2,1)} async-done(((bf16[512,512]{1,0:T(8,128)(2,1)}), bf16[512,2048]{1,0:T(8,128)(2,1)}) %all-gather.7.cloned.1.call-update) | async-done | bytes 2097168 | tf_op jit(solution)/shard_map/all_gather | solution.py:44
  104.0 2.9 convolution_convert_fusion.2
  108.0 32.0 %reduce-scatter.4.cloned.1.call-done = bf16[128,256]{1,0:T(8,128)(2,1)} async-done(((bf16[128,2048]{1,0:T(8,128)(2,1)}), bf16[128,256]{1,0:T(8,128)(2,1)}) %reduce-scatter.4.cloned.1.call-update) | async-done | bytes 65552 | tf_op jit(solution)/shard_map/reduce_scatter | solution.py:72
  141.1 1.2 collective-permute-done.3
  142.4 1.5 collective-permute-start.4
  144.0 4.1 %collective-permute-done.4 = bf16[128,512]{1,0:T(8,128)(2,1)S(1)} collective-permute-done((bf16[128,512]{1,0:T(8,128)(2,1)S(1)}, bf16[128,512]{1,0:T(8,128)(2,1)S(1)}, u32[]{:S(2)}, u32[]{:S(2)}) %collective-permute-start.4) | collective-permute-done | bytes 131104 | tf_op jit(solution)/shard_map/ppermute | solution.py:60
  148.1 1.5 collective-permute-start.5
  149.9 5.8 %collective-permute-done.5 = bf16[128,1024]{1,0:T(8,128)(2,1)S(1)} collective-permute-done((bf16[128,1024]{1,0:T(8,128)(2,1)S(1)}, bf16[128,1024]{1,0:T(8,128)(2,1)S(1)}, u32[]{:S(2)}, u32[]{:S(2)}) %collective-permute-start.5) | collective-permute-done | bytes 262176 | tf_op jit(solution)/shard_map/ppermute | solution.py:60
  157.1 1.3 convolution_convert_fusion.1
  158.6 2.0 maximum_select_fusion.3
  160.6 32.1 %reduce-scatter.6.cloned.1.call-done = bf16[128,256]{1,0:T(8,128)(2,1)} async-done(((bf16[128,2048]{1,0:T(8,128)(2,1)}), bf16[128,256]{1,0:T(8,128)(2,1)}) %reduce-scatter.6.cloned.1.call-update) | async-done | bytes 65552 | tf_op jit(solution)/shard_map/reduce_scatter | solution.py:72
  193.7 12.2 %all-reduce = (f32[128]{0:T(128)S(1)}, f32[128]{0:T(128)S(1)}, f32[128]{0:T(128)S(1)}, f32[128]{0:T(128)S(1)}, f32[128]{0:T(128)S(1)}, /*index=5*/f32[128]{0:T(128)S(1)}) all-reduce(f32[128]{0:T(128)S(1)} %get-tuple-element.5, f32[128]{0:T(128)S(1)} %get-tuple-element.6, ...), channel_id=1, replica_groups=mesh['row'=4,'col'=8] {'col'}, use_global_device_ids=true, to_apply=%region_7.8 | all-reduce | flops 768 | bytes 6144 | tf_op jit(solution)/shard_map/psum | solution.py:27
  206.9 10.9 %all_gather.20 = bf16[128,2048]{1,0:T(8,128)(2,1)S(1)} all-gather(bf16[128,256]{1,0:T(8,128)(2,1)S(1)} %fusion.20), channel_id=1, replica_groups=mesh['row'=4,'col'=8] {'col'}, dimensions={1}, use_global_device_ids=true | all-gather | bytes 589824 | tf_op jit(solution)/shard_map/all_gather | solution.py:85
  217.8 2.4 fusion
  220.2 1.6 convolution_convert_fusion
  223.0 2.0 copy.11
  225.0 4.8 %all-to-all-start = ((bf16[2,128,2048]{1,0,2:T(2,128)(2,1)}), bf16[2,128,2048]{1,0,2:T(2,128)(2,1)S(1)}, u32[]{:S(2)}, u32[]{:S(2)}) async-start(bf16[2,128,2048]{1,0,2:T(2,128)(2,1)} %copy.11), calls=%async_computation.1 | async-start | bytes 2097152 | tf_op jit(solution)/shard_map/all_to_all | solution.py:111
  230.7 25.6 %reduce-scatter.8.cloned.1.call-done = bf16[128,256]{1,0:T(8,128)(2,1)} async-done(((bf16[128,2048]{1,0:T(8,128)(2,1)}), bf16[128,256]{1,0:T(8,128)(2,1)}) %reduce-scatter.8.cloned.1.call-update) | async-done | bytes 65552 | tf_op jit(solution)/shard_map/reduce_scatter | solution.py:96
  257.3 10.9 %all_gather.21 = bf16[128,2048]{1,0:T(8,128)(2,1)S(1)} all-gather(bf16[128,256]{1,0:T(8,128)(2,1)S(1)} %fusion.28), channel_id=1, replica_groups=mesh['row'=4,'col'=8] {'col'}, dimensions={1}, use_global_device_ids=true | all-gather | bytes 589824 | tf_op jit(solution)/shard_map/all_gather | solution.py:85
  268.3 2.0 copy.13
  270.3 4.6 %all-to-all-start.1 = ((bf16[2,128,2048]{1,0,2:T(2,128)(2,1)}), bf16[2,128,2048]{1,0,2:T(2,128)(2,1)S(1)}, u32[]{:S(2)}, u32[]{:S(2)}) async-start(bf16[2,128,2048]{1,0,2:T(2,128)(2,1)} %copy.13), calls=%async_computation.4 | async-start | bytes 2097152 | tf_op jit(solution)/shard_map/all_to_all | solution.py:106
  274.9 2.4 fusion.2
  279.4 33.5 %all-to-all-done.1 = bf16[2,128,2048]{1,0,2:T(2,128)(2,1)S(1)} async-done(((bf16[2,128,2048]{1,0,2:T(2,128)(2,1)}), bf16[2,128,2048]{1,0,2:T(2,128)(2,1)S(1)}, u32[]{:S(2)}, u32[]{:S(2)}) %all-to-all-start.1) | async-done | bytes 1048608 | tf_op jit(solution)/shard_map/all_to_all | solution.py:106
  313.7 2.9 convolution_bitcast_fusion
  316.6 9.0 %all-gather.9.cloned.1.call-done = bf16[2,512,512]{2,1,0:T(8,128)(2,1)} async-done(((bf16[2,128,512]{2,1,0:T(8,128)(2,1)}), bf16[2,512,512]{2,1,0:T(8,128)(2,1)}) %all-gather.9.cloned.1.call-update) | async-done | bytes 1048592 | tf_op jit(solution)/shard_map/all_gather | solution.py:114
  325.5 2.9 convolution_bitcast_fusion.1
  (68 shorter events, 17.3 us)
Async XLA Ops:
  7.2 13.6 %copy-start = (bf16[18,512]{1,0:T(8,128)(2,1)S(1)}, bf16[18,512]{1,0:T(8,128)(2,1)}, u32[]{:S(2)}) copy-start(bf16[18,512]{1,0:T(8,128)(2,1)} %param.11) | copy-start | bytes 55300
  7.2 50.8 %all-gather.5.cloned.1.call-start = ((), (), s32[]{:S(2)}) async-start(), calls=%async_computation.5 | async-start | bytes 2621440 | tf_op jit(solution)/shard_map/all_gather | solution.py:43
  7.9 96.1 %all-gather.7.cloned.1.call-start = ((), (), s32[]{:S(2)}) async-start(), calls=%async_computation.6 | async-start | bytes 2621440 | tf_op jit(solution)/shard_map/all_gather | solution.py:44
  8.7 131.4 %reduce-scatter.4.cloned.1.call-start = ((), (), s32[]{:S(2)}) async-start(), calls=%async_computation.7 | async-start | bytes 589824 | tf_op jit(solution)/shard_map/reduce_scatter | solution.py:72
  8.7 1.7 collective-permute-start
  11.3 6.7 %collective-permute-start.1 = (bf16[128,512]{1,0:T(8,128)(2,1)S(1)}, bf16[128,512]{1,0:T(8,128)(2,1)S(1)}, u32[]{:S(2)}, u32[]{:S(2)}) collective-permute-start(bf16[128,512]{1,0:T(8,128)(2,1)S(1)} %maximum_select_fusion.8), channel_id=1, source_target_pairs={{0,2},{1,3},{2,0},{3,1},{4,6},{5,7},{6,4},{7,5},{8,10},{9,11},{10,... | collective-permute-start | bytes 393224 | tf_op jit(solution)/shard_map/ppermute | solution.py:60
  18.1 7.9 %collective-permute-start.2 = (bf16[128,1024]{1,0:T(8,128)(2,1)S(1)}, bf16[128,1024]{1,0:T(8,128)(2,1)S(1)}, u32[]{:S(2)}, u32[]{:S(2)}) collective-permute-start(bf16[128,1024]{1,0:T(8,128)(2,1)S(1)} %maximum_select_fusion.6), channel_id=1, source_target_pairs={{0,4},{1,5},{2,6},{3,7},{4,0},{5,1},{6,2},{7,3},{8,12},{9,13},{10,... | collective-permute-start | bytes 786440 | tf_op jit(solution)/shard_map/ppermute | solution.py:60
  26.0 78.0 %copy-start.8 = (bf16[128,1024]{1,0:T(8,128)(2,1)}, bf16[128,1024]{1,0:T(8,128)(2,1)S(1)}, u32[]{:S(2)}) copy-start(bf16[128,1024]{1,0:T(8,128)(2,1)S(1)} %collective-permute-done.2) | copy-start | bytes 786436
  60.0 44.0 %copy-start.3 = (f32[128,512]{1,0:T(8,128)}, f32[128,512]{1,0:T(8,128)S(1)}, u32[]{:S(2)}) copy-start(f32[128,512]{1,0:T(8,128)S(1)} %convolution_add_fusion.1) | copy-start | bytes 786436
  60.0 47.0 %copy-start.2 = (bf16[2,128,2048]{2,1,0:T(8,128)(2,1)S(1)}, bf16[2,128,2048]{2,1,0:T(8,128)(2,1)}, u32[]{:S(2)}) copy-start(bf16[2,128,2048]{2,1,0:T(8,128)(2,1)} %param.8) | copy-start | bytes 3145732
  106.9 48.8 %copy-start.1 = (bf16[2048,512]{1,0:T(8,128)(2,1)S(1)}, bf16[2048,512]{1,0:T(8,128)(2,1)}, u32[]{:S(2)}) copy-start(bf16[2048,512]{1,0:T(8,128)(2,1)} %all-gather.5.cloned.1.call-done) | copy-start | bytes 6291460
  106.9 85.7 %reduce-scatter.6.cloned.1.call-start = ((), (), s32[]{:S(2)}) async-start(), calls=%async_computation.8 | async-start | bytes 589824 | tf_op jit(solution)/shard_map/reduce_scatter | solution.py:72
  141.1 1.3 collective-permute-start.3
  142.4 5.6 %collective-permute-start.4 = (bf16[128,512]{1,0:T(8,128)(2,1)S(1)}, bf16[128,512]{1,0:T(8,128)(2,1)S(1)}, u32[]{:S(2)}, u32[]{:S(2)}) collective-permute-start(bf16[128,512]{1,0:T(8,128)(2,1)S(1)} %maximum_select_fusion.9), channel_id=1, source_target_pairs={{0,2},{1,3},{2,0},{3,1},{4,6},{5,7},{6,4},{7,5},{8,10},{9,11},{10,... | collective-permute-start | bytes 393224 | tf_op jit(solution)/shard_map/ppermute | solution.py:60
  148.1 7.6 %collective-permute-start.5 = (bf16[128,1024]{1,0:T(8,128)(2,1)S(1)}, bf16[128,1024]{1,0:T(8,128)(2,1)S(1)}, u32[]{:S(2)}, u32[]{:S(2)}) collective-permute-start(bf16[128,1024]{1,0:T(8,128)(2,1)S(1)} %maximum_select_fusion.7), channel_id=1, source_target_pairs={{0,4},{1,5},{2,6},{3,7},{4,0},{5,1},{6,2},{7,3},{8,12},{9,13},{10,... | collective-permute-start | bytes 786440 | tf_op jit(solution)/shard_map/ppermute | solution.py:60
  149.9 7.2 %copy-start.11 = (bf16[512,2048]{1,0:T(8,128)(2,1)S(1)}, bf16[512,2048]{1,0:T(8,128)(2,1)}, u32[]{:S(2)}) copy-start(bf16[512,2048]{1,0:T(8,128)(2,1)} %all-gather.7.cloned.1.call-done) | copy-start | bytes 6291460
  155.7 0.7 copy-start.10
  156.4 0.7 copy-start.6
  157.1 1.3 copy-start.9
  158.4 97.9 %reduce-scatter.8.cloned.1.call-start = ((), (), s32[]{:S(2)}) async-start(), calls=%async_computation.9 | async-start | bytes 589824 | tf_op jit(solution)/shard_map/reduce_scatter | solution.py:96
  223.0 6.8 %copy-start.4 = (f32[128,512]{1,0:T(8,128)S(1)}, f32[128,512]{1,0:T(8,128)}, u32[]{:S(2)}) copy-start(f32[128,512]{1,0:T(8,128)} %copy-done.3) | copy-start | bytes 786436
  223.0 6.9 %copy-start.7 = (f32[128,512]{1,0:T(8,128)S(1)}, f32[128,512]{1,0:T(8,128)}, u32[]{:S(2)}) copy-start(f32[128,512]{1,0:T(8,128)} %copy-done.6) | copy-start | bytes 786436
  225.0 45.3 %all-to-all-start = ((bf16[2,128,2048]{1,0,2:T(2,128)(2,1)}), bf16[2,128,2048]{1,0,2:T(2,128)(2,1)S(1)}, u32[]{:S(2)}, u32[]{:S(2)}) async-start(bf16[2,128,2048]{1,0,2:T(2,128)(2,1)} %copy.11), calls=%async_computation.1 | async-start | bytes 2097152 | tf_op jit(solution)/shard_map/all_to_all | solution.py:111
  229.8 83.9 %all-gather.11.cloned.1.call-start = ((), (), s32[]{:S(2)}) async-start(), calls=%async_computation.11 | async-start | bytes 1310720 | tf_op jit(solution)/shard_map/all_gather | solution.py:107
  268.3 6.6 %copy-start.5 = (f32[128,512]{1,0:T(8,128)S(1)}, f32[128,512]{1,0:T(8,128)}, u32[]{:S(2)}) copy-start(f32[128,512]{1,0:T(8,128)} %copy-done.3) | copy-start | bytes 786436
  270.3 42.6 %all-to-all-start.1 = ((bf16[2,128,2048]{1,0,2:T(2,128)(2,1)}), bf16[2,128,2048]{1,0,2:T(2,128)(2,1)S(1)}, u32[]{:S(2)}, u32[]{:S(2)}) async-start(bf16[2,128,2048]{1,0,2:T(2,128)(2,1)} %copy.13), calls=%async_computation.4 | async-start | bytes 2097152 | tf_op jit(solution)/shard_map/all_to_all | solution.py:106
  274.9 50.7 %all-gather.9.cloned.1.call-start = ((), (), s32[]{:S(2)}) async-start(), calls=%async_computation.10 | async-start | bytes 1310720 | tf_op jit(solution)/shard_map/all_gather | solution.py:114
Sparse Core Ops, SparseCore 0:
  9.6 48.3 all-gather.4
  59.5 44.4 all-gather.6
  107.1 32.8 reduce-scatter.3
  158.5 34.0 reduce-scatter.5
  222.0 34.2 reduce-scatter.7
  257.7 37.5 all-gather.10
  296.8 28.6 all-gather.8
